TPU v7x, 256 devices: a whole 4x4x8 slice. The times are simulated.
256 devices in a mesh: grp: 8 (over z), ep: 32 (over y, x, core).
Axes of the slice: x: 4, y: 4, z: 8, core: 2. Of those that a mesh axis runs over, the one named last changes fastest.
Arguments:
- pol_hidden: bfloat16 [10240, 1024], P(('grp', 'ep')), may hold values from -80 to 80
- ref_hidden: bfloat16 [10240, 1024], P(('grp', 'ep')), may hold values from -80 to 80
- pol_routes: int32 [10240, 8], P(('grp', 'ep')), may hold values from 0 to 63, all different within a row; in each aligned block of 40 rows (0 to 39, 40 to 79, ...) at most 7 rows name the same one
- ref_routes: int32 [10240, 8], P(('grp', 'ep')), may hold values from 0 to 63, all different within a row; in each aligned block of 40 rows (0 to 39, 40 to 79, ...) at most 7 rows name the same one
- pol_gates: float32 [10240, 8], P(('grp', 'ep')), may hold values from 0.02 to 0.3
- ref_gates: float32 [10240, 8], P(('grp', 'ep')), may hold values from 0.02 to 0.3
- w_gate: bfloat16 [64, 1024, 384], P('ep'), may hold values from -0.1875 to 0.1875
- w_up: bfloat16 [64, 1024, 384], P('ep'), may hold values from -0.1875 to 0.1875
- w_down: bfloat16 [64, 384, 1024], P('ep'), may hold values from -0.3125 to 0.3125
- norm_gain: float32 [1024], replicated, may hold values from 0.5 to 1.5
- vocab_head: bfloat16 [77824, 1024], P(('grp', 'ep')), may hold values from -2 to 2
- targets: int32 [10240], P(('grp', 'ep')), may hold values from 0 to 77823
- seq_lengths: int32 [256], replicated, may hold values from 1 to 1024, 10240 in all
- owners: int32 [256], replicated, may hold values from 0 to 255, each once
Outputs:
- token_ratio: float32 [10240], P(('grp', 'ep'))
- owned_mean: float32 [256], P(('grp', 'ep'))
Inputs may be any that keep to these rules, and one draw needn't show every extreme that they name: `pol_routes`: each row names 8 different experts; among the 40 rows of one device no expert is named by more than 7 rows, a bound that some block reaches. `ref_routes`: each row names 8 different experts; among the 40 rows of one device no expert is named by more than 7 rows, a bound that some block reaches. `seq_lengths`: the lengths sum to 10240; the longest is exactly 1024. `owners`: every device index appears exactly once.
All inputs are finite; a program needn't handle non-finite values.
Results may differ from a plain program's by a relative error of at most 0.0062.
Values may be sent and summed in bfloat16 or wider, within the bound.
A program may use at most 128 MiB of HBM per device.

v0:
```python
import jax
import jax.numpy as jnp
from jax import lax
from jax.sharding import PartitionSpec as P


def joined_2(value, axis, join):
    pieces = jax.tree.map(lambda part: lax.all_gather(part, axis), value)
    head = jax.tree.map(lambda part: part[0], pieces)
    tail = jax.tree.map(lambda part: part[1:], pieces)
    so_far, _ = lax.scan(lambda so_far, share: (join(so_far, share), None), head, tail)
    return so_far


def combine_stats(earlier_part, second):
    peak = jnp.maximum(earlier_part[0], second[0])
    totals = earlier_part[1] * jnp.exp(earlier_part[0] - peak) + second[1] * jnp.exp(
        second[0] - peak
    )
    return (peak, totals, earlier_part[2] + second[2])


def vocab_stats(row_block, weights, vocab_ids, wanted):
    logits = jnp.einsum("td,vd->tv", row_block, weights, preferred_element_type=jnp.float32)
    peak = jnp.max(logits, axis=1)
    totals = jnp.sum(jnp.exp(logits - peak[:, None]), axis=1)
    picked = jnp.sum(jnp.where(vocab_ids[None, :] == wanted[:, None], logits, 0.0), axis=1)
    return (peak, totals, picked)


def expert_tables(routes, gates, experts, capacity):
    route_hits = routes[:, :, None] == jnp.arange(experts, dtype=jnp.int32)[None, None, :]
    members = jnp.sum(route_hits.astype(jnp.int32), axis=1)
    earlier = jnp.cumsum(members, axis=0) - members
    placed = (members[:, :, None] > 0) & (
        earlier[:, :, None] == jnp.arange(capacity, dtype=jnp.int32)[None, None, :]
    )
    weight = jnp.sum(jnp.where(route_hits, gates[:, :, None], 0.0), axis=1)
    tok_count = routes.shape[0]
    picker = placed.astype(jnp.bfloat16).reshape(tok_count, experts * capacity)
    mixing = (weight[:, :, None] * placed.astype(jnp.float32)).reshape(
        tok_count, experts * capacity
    )
    return (picker, mixing)


def local(
    pol_hidden,
    ref_hidden,
    pol_routes,
    ref_routes,
    pol_gates,
    ref_gates,
    w_gate,
    w_up,
    w_down,
    norm_gain,
    vocab_head,
    targets,
    seq_lengths,
    owners,
):
    groups = lax.axis_size("ep")
    device_index = lax.axis_index(("grp", "ep"))
    local_experts = w_gate.shape[0]
    experts = local_experts * groups
    tok_count = pol_hidden.shape[0]
    width = pol_hidden.shape[1]
    fanout = pol_routes.shape[1]
    capacity = tok_count * fanout // experts + 2
    pol_pick, pol_mixing = expert_tables(pol_routes, pol_gates, experts, capacity)
    ref_pick, ref_mixing = expert_tables(ref_routes, ref_gates, experts, capacity)
    pol_send = jnp.einsum(
        "ts,td->sd", pol_pick, pol_hidden, preferred_element_type=jnp.float32
    ).astype(jnp.bfloat16)
    ref_send = jnp.einsum(
        "ts,td->sd", ref_pick, ref_hidden, preferred_element_type=jnp.float32
    ).astype(jnp.bfloat16)
    pol_send = pol_send.reshape(groups, local_experts, capacity, width)
    ref_send = ref_send.reshape(groups, local_experts, capacity, width)
    pol_part = lax.all_to_all(pol_send, "ep", split_axis=0, concat_axis=0, tiled=True)
    ref_part = lax.all_to_all(ref_send, "ep", split_axis=0, concat_axis=0, tiled=True)
    slots = pol_part.shape[2]
    joined = jnp.concatenate((pol_part, ref_part), axis=2)
    gate_act = jnp.einsum("nesd,edf->nesf", joined, w_gate, preferred_element_type=jnp.float32)
    up_act = jnp.einsum("nesd,edf->nesf", joined, w_up, preferred_element_type=jnp.float32)
    inner = (jax.nn.silu(gate_act) * up_act).astype(jnp.bfloat16)
    outputs = jnp.einsum(
        "nesf,efd->nesd", inner, w_down, preferred_element_type=jnp.float32
    ).astype(jnp.bfloat16)
    pol_back = lax.all_to_all(outputs[:, :, :slots], "ep", split_axis=0, concat_axis=0, tiled=True)
    ref_back = lax.all_to_all(outputs[:, :, slots:], "ep", split_axis=0, concat_axis=0, tiled=True)

    def mix_back(hidden, mixing, back):
        rows_back = back.reshape(experts * capacity, width).astype(jnp.float32)
        mixed = hidden.astype(jnp.float32) + jnp.dot(
            mixing, rows_back, precision=lax.Precision.HIGHEST
        )
        scale = lax.rsqrt(jnp.mean(mixed * mixed, axis=1, keepdims=True) + 1e-06)
        return (mixed * scale * norm_gain).astype(jnp.bfloat16)

    pol_normed = mix_back(pol_hidden, pol_mixing, pol_back)
    ref_normed = mix_back(ref_hidden, ref_mixing, ref_back)
    vocab_rows = vocab_head.shape[0]
    band = lax.axis_index("grp")
    pol_col, ref_col, wanted = (
        lax.all_gather(pol_normed, "grp", axis=0, tiled=True),
        lax.all_gather(ref_normed, "grp", axis=0, tiled=True),
        lax.all_gather(targets, "grp", axis=0, tiled=True),
    )
    col_count = wanted.shape[0]
    floor_value = jnp.full((2, col_count), -1e30, jnp.float32)
    blank = jnp.zeros((2, col_count), jnp.float32)
    piece = lax.all_gather(vocab_head, "ep", axis=0, tiled=True)
    count = piece.shape[0]
    place = jnp.arange(count, dtype=jnp.int32)
    vocab_ids = band * groups * vocab_rows + place
    pol_stats = vocab_stats(pol_col, piece, vocab_ids, wanted)
    ref_stats = vocab_stats(ref_col, piece, vocab_ids, wanted)
    fresh = tuple(
        (jnp.stack((pol_part, ref_part)) for pol_part, ref_part in zip(pol_stats, ref_stats))
    )
    stats = combine_stats((floor_value, blank, blank), fresh)
    peak, totals, picked = joined_2(stats, "grp", combine_stats)
    logprob = picked - (peak + jnp.log(totals))
    mine = lax.dynamic_slice_in_dim(logprob, band * tok_count, tok_count, axis=1)
    token_ratio = mine[0] - mine[1]
    offsets = jnp.cumsum(seq_lengths) - seq_lengths
    positions = device_index * tok_count + jnp.arange(tok_count, dtype=jnp.int32)
    inside = (positions[:, None] >= offsets[None, :]) & (
        positions[:, None] < (offsets + seq_lengths)[None, :]
    )
    partial_value = jnp.dot(
        token_ratio, inside.astype(jnp.float32), precision=lax.Precision.HIGHEST
    ) / seq_lengths.astype(jnp.float32)
    sums = lax.psum(partial_value, ("grp", "ep"))
    owned = jnp.sum(jnp.where(owners == device_index, sums, 0.0)).reshape(1)
    return (token_ratio, owned)


def solution(mesh):
    return jax.shard_map(
        local,
        mesh=mesh,
        in_specs=(
            P(("grp", "ep"), None),
            P(("grp", "ep"), None),
            P(("grp", "ep"), None),
            P(("grp", "ep"), None),
            P(("grp", "ep"), None),
            P(("grp", "ep"), None),
            P("ep", None, None),
            P("ep", None, None),
            P("ep", None, None),
            P(),
            P(("grp", "ep"), None),
            P(("grp", "ep")),
            P(),
            P(),
        ),
        out_specs=(P(("grp", "ep")), P(("grp", "ep"))),
        check_vma=False,
    )
```

profile of v0, /device:TPU:1, one launch (start us, length us, event | category | flops | bytes accessed | tf_op | source)
XLA Modules:
  0.0 389.7 jit_solution(15554492775969641314)
XLA Ops:
  7.2 0.7 all-gather.4.cloned.1.call-update
  7.9 0.8 copy.62
  8.9 0.4 copy-done.13
  9.4 0.6 copy-done.9
  10.4 0.6 copy-done.18
  11.0 0.4 convolution_convert_fusion.1
  11.8 2.0 copy.67
  13.7 8.7 %all-to-all-start = ((bf16[32,2,7,1024]{3,1,2,0:T(2,128)(2,1)}), bf16[32,2,7,1024]{3,1,2,0:T(2,128)(2,1)S(1)}, u32[]{:S(2)}, u32[]{:S(2)}) async-start(bf16[32,2,7,1024]{3,1,2,0:T(2,128)(2,1)} %copy.67), calls=%async_computation | async-start | bytes 1835008 | tf_op jit(solution)/shard_map/all_to_all | solution.py:81
  22.7 0.4 copy-done.15
  23.2 0.6 copy-done.11
  24.1 1.4 convolution_convert_fusion
  25.5 1.4 reshape.318
  27.0 2.0 copy.71
  28.9 12.9 %all-to-all-done = bf16[32,2,7,1024]{3,1,2,0:T(2,128)(2,1)S(1)} async-done(((bf16[32,2,7,1024]{3,1,2,0:T(2,128)(2,1)}), bf16[32,2,7,1024]{3,1,2,0:T(2,128)(2,1)S(1)}, u32[]{:S(2)}, u32[]{:S(2)}) %all-to-all-start) | async-done | bytes 917536 | tf_op jit(solution)/shard_map/all_to_all | solution.py:81
  41.8 0.9 copy-done.2
  42.7 5.4 %all-to-all-start.1 = ((bf16[32,2,7,1024]{3,1,2,0:T(2,128)(2,1)}), bf16[32,2,7,1024]{3,1,2,0:T(2,128)(2,1)}, u32[]{:S(2)}, u32[]{:S(2)}) async-start(bf16[32,2,7,1024]{3,1,2,0:T(2,128)(2,1)} %copy.71), calls=%async_computation.1 | async-start | bytes 1835008 | tf_op jit(solution)/shard_map/all_to_all | solution.py:82
  48.2 1.4 copy_dynamic-update-slice_fusion.1
  49.6 14.5 %all-to-all-done.1 = bf16[32,2,7,1024]{3,1,2,0:T(2,128)(2,1)} async-done(((bf16[32,2,7,1024]{3,1,2,0:T(2,128)(2,1)}), bf16[32,2,7,1024]{3,1,2,0:T(2,128)(2,1)}, u32[]{:S(2)}, u32[]{:S(2)}) %all-to-all-start.1) | async-done | bytes 917536 | tf_op jit(solution)/shard_map/all_to_all | solution.py:82
  64.1 1.5 copy_dynamic-update-slice_fusion
  65.8 2.2 fusion.9
  68.0 5.2 %convert_bitcast_fusion = bf16[32,2,14,1024]{3,0,2,1:T(8,128)(2,1)} fusion(bf16[2,384,1024]{2,1,0:T(8,128)(2,1)S(1)} %copy-done, bf16[32,2,14,1024]{3,0,2,1:T(8,128)(2,1)S(1)} %copy_dynamic-update-slice_fusion, bf16[2,1024,384]{2,1,0:T(8,128)(2,1)} %param.23, f32[32,2,14,384]{3,0,2,1:T(8,128)} %fusion.9), kind=kOutput, calls=%fused_computation.12 | convolution fusion | flops 1412268032 | bytes 8192000 | tf_op jit(solution)/shard_map/nesf,efd->nesd/dot_general | solution.py:88
  73.2 1.9 fusion.44
  75.2 1.9 copy.78
  77.1 3.9 all-to-all-start.3
  81.8 1.9 copy.74
  83.7 21.1 %all-to-all-done.3 = bf16[32,2,7,1024]{3,1,2,0:T(2,128)(2,1)S(1)} async-done(((bf16[32,2,7,1024]{3,1,2,0:T(2,128)(2,1)}), bf16[32,2,7,1024]{3,1,2,0:T(2,128)(2,1)S(1)}, u32[]{:S(2)}, u32[]{:S(2)}) %all-to-all-start.3) | async-done | bytes 917536 | tf_op jit(solution)/shard_map/all_to_all | solution.py:92
  104.8 6.1 %all-to-all-start.2 = ((bf16[32,2,7,1024]{3,1,2,0:T(2,128)(2,1)}), bf16[32,2,7,1024]{3,1,2,0:T(2,128)(2,1)S(1)}, u32[]{:S(2)}, u32[]{:S(2)}) async-start(bf16[32,2,7,1024]{3,1,2,0:T(2,128)(2,1)} %copy.74), calls=%async_computation.2 | async-start | bytes 1835008 | tf_op jit(solution)/shard_map/all_to_all | solution.py:91
  111.0 0.7 mul.94
  112.2 0.6 dynamic-slice
  113.7 20.4 %all-reduce = s32[320]{0:T(512)S(1)} all-reduce(s32[320]{0:T(512)S(1)} %dynamic-update-slice), channel_id=1, replica_groups=mesh['grp'=8,'ep'=32] {'grp'}, use_global_device_ids=true, to_apply=%add | all-reduce | flops 320 | bytes 2560
  134.0 0.6 iota_add_fusion.1
  134.7 0.6 fusion.43
  135.4 0.6 iota_add_fusion
  136.3 1.2 reshape.320
  138.1 0.6 copy-done.3
  138.7 0.7 multiply_reduce_fusion
  139.4 1.7 multiply_reduce_fusion.1
  141.2 20.2 %all_gather.26 = bf16[320,1024]{1,0:T(8,128)(2,1)S(1)} all-gather(bf16[40,1024]{1,0:T(8,128)(2,1)S(1)} %get-tuple-element.71), channel_id=1, replica_groups=mesh['grp'=8,'ep'=32] {'grp'}, dimensions={0}, use_global_device_ids=true | all-gather | bytes 737280 | tf_op jit(solution)/shard_map/all_gather | solution.py:107
  161.4 20.5 %all_gather.28 = bf16[320,1024]{1,0:T(8,128)(2,1)S(1)} all-gather(bf16[40,1024]{1,0:T(8,128)(2,1)S(1)} %get-tuple-element.72), channel_id=1, replica_groups=mesh['grp'=8,'ep'=32] {'grp'}, dimensions={0}, use_global_device_ids=true | all-gather | bytes 737280 | tf_op jit(solution)/shard_map/all_gather | solution.py:108
  181.9 13.4 %fusion.45 = (f32[320]{0:T(512)S(1)}, f32[320,9728]{1,0:T(8,128)}) fusion(bf16[320,1024]{1,0:T(8,128)(2,1)S(1)} %all_gather.26, bf16[9728,1024]{1,0:T(8,128)(2,1)} %all-gather.4.cloned.1.call-done), kind=kOutput, calls=%fused_computation.84 | convolution fusion | flops 6378454528 | bytes 33031424 | tf_op jit(solution)/shard_map/td,vd->tv/dot_general | solution.py:24
  195.3 13.5 %fusion.46 = (f32[320]{0:T(512)S(1)}, f32[320,9728]{1,0:T(8,128)}) fusion(bf16[320,1024]{1,0:T(8,128)(2,1)S(1)} %all_gather.28, bf16[9728,1024]{1,0:T(8,128)(2,1)} %all-gather.4.cloned.1.call-done), kind=kOutput, calls=%fused_computation.85 | convolution fusion | flops 6378454528 | bytes 33031424 | tf_op jit(solution)/shard_map/td,vd->tv/dot_general | solution.py:24
  208.8 11.5 %fusion.2 = (f32[320]{0:T(512)S(1)}, f32[320]{0:T(512)S(1)}, f32[320]{0:T(512)S(1)}, f32[320]{0:T(512)S(1)}) fusion(f32[320,9728]{1,0:T(8,128)} %get-tuple-element.80, s32[9728]{0:T(1024)S(1)} %copy-done.17, s32[320]{0:T(512)S(1)} %all-reduce, f32[320]{0:T(512)S(1)} %get-tuple-element.79, f32[320,9728]{1,0:T(8,128)} %get-tuple-element.82, ...), kind=kLoop, calls=%fused_computation.8 | loop fusion | flops 28015360 | bytes 24951552 | tf_op jit(solution)/shard_map/reduce_sum | solution.py:27
  220.3 18.0 %all-gather.1 = f32[8,2,320]{2,1,0:T(2,128)S(1)} all-gather(f32[1,2,320]{2,1,0:T(2,128)S(1)} %maximum_bitcast_fusion), channel_id=2, replica_groups=mesh['grp'=8,'ep'=32] {'grp'}, dimensions={0}, use_global_device_ids=true | all-gather | bytes 23040 | tf_op jit(solution)/shard_map/all_gather | solution.py:8
  238.4 18.0 %all_gather.30 = f32[8,2,320]{2,1,0:T(2,128)S(1)} all-gather(f32[1,2,320]{2,1,0:T(2,128)S(1)} %get-tuple-element.73), channel_id=1, replica_groups=mesh['grp'=8,'ep'=32] {'grp'}, dimensions={0}, use_global_device_ids=true | all-gather | bytes 23040 | tf_op jit(solution)/shard_map/all_gather | solution.py:8
  256.5 18.0 %all_gather.29 = f32[8,2,320]{2,1,0:T(2,128)S(1)} all-gather(f32[1,2,320]{2,1,0:T(2,128)S(1)} %get-tuple-element.74), channel_id=1, replica_groups=mesh['grp'=8,'ep'=32] {'grp'}, dimensions={0}, use_global_device_ids=true | all-gather | bytes 23040 | tf_op jit(solution)/shard_map/all_gather | solution.py:8
  274.9 0.5 fusion.42
  275.7 106.6 %psum.7 = f32[256]{0:T(256)S(1)} all-reduce(f32[256]{0:T(256)S(1)} %convert_divide_fusion), channel_id=1, replica_groups=mesh['grp'=8,'ep'=32] {'grp','ep'}, use_global_device_ids=true, to_apply=%region_18.19 | all-reduce | flops 256 | bytes 2048 | tf_op jit(solution)/shard_map/psum | solution.py:136
  382.2 0.6 fusion.39
  (125 shorter events, 5.3 us)
Async XLA Ops:
  7.2 60.8 %copy-start = (bf16[2,384,1024]{2,1,0:T(8,128)(2,1)S(1)}, bf16[2,384,1024]{2,1,0:T(8,128)(2,1)}, u32[]{:S(2)}) copy-start(bf16[2,384,1024]{2,1,0:T(8,128)(2,1)} %param.24) | copy-start | bytes 4718596
  7.2 3.8 copy-start.7
  7.2 174.7 %all-gather.4.cloned.1.call-start = ((), (), s32[]{:S(2)}) async-start(), calls=%async_computation.4 | async-start | bytes 20545536 | tf_op jit(solution)/shard_map/all_gather | solution.py:114
  8.7 0.6 copy-start.13
  9.4 0.6 copy-start.9
  10.4 0.6 copy-start.18
  11.7 10.7 %copy-start.22 = (s32[40,8]{0,1:T(8,128)S(1)}, s32[40,8]{0,1:T(8,128)}, u32[]{:S(2)}) copy-start(s32[40,8]{0,1:T(8,128)} %param.19) | copy-start | bytes 3844
  13.7 10.4 %copy-start.5 = (bf16[40,1024]{1,0:T(8,128)(2,1)S(1)}, bf16[40,1024]{1,0:T(8,128)(2,1)}, u32[]{:S(2)}) copy-start(bf16[40,1024]{1,0:T(8,128)(2,1)} %param.17) | copy-start | bytes 245764
  13.7 10.4 %copy-start.19 = (s32[448]{0:T(512)S(1)}, s32[448]{0:T(512)}, u32[]{:S(2)}) copy-start(s32[448]{0:T(512)} %copy-done.18) | copy-start | bytes 5380
  13.7 28.1 %all-to-all-start = ((bf16[32,2,7,1024]{3,1,2,0:T(2,128)(2,1)}), bf16[32,2,7,1024]{3,1,2,0:T(2,128)(2,1)S(1)}, u32[]{:S(2)}, u32[]{:S(2)}) async-start(bf16[32,2,7,1024]{3,1,2,0:T(2,128)(2,1)} %copy.67), calls=%async_computation | async-start | bytes 1835008 | tf_op jit(solution)/shard_map/all_to_all | solution.py:81
  22.5 0.6 copy-start.15
  23.2 0.6 copy-start.11
  41.8 0.9 copy-start.2
  42.7 21.4 %all-to-all-start.1 = ((bf16[32,2,7,1024]{3,1,2,0:T(2,128)(2,1)}), bf16[32,2,7,1024]{3,1,2,0:T(2,128)(2,1)}, u32[]{:S(2)}, u32[]{:S(2)}) async-start(bf16[32,2,7,1024]{3,1,2,0:T(2,128)(2,1)} %copy.71), calls=%async_computation.1 | async-start | bytes 1835008 | tf_op jit(solution)/shard_map/all_to_all | solution.py:82
  64.1 1.7 copy-start.4
  75.2 5.8 %copy-start.23 = (f32[40,8]{0,1:T(8,128)S(1)}, f32[40,8]{0,1:T(8,128)}, u32[]{:S(2)}) copy-start(f32[40,8]{0,1:T(8,128)} %param.21) | copy-start | bytes 3844
  75.2 5.9 %copy-start.16 = (s32[40,8]{1,0:T(8,128)S(1)}, s32[40,8]{1,0:T(8,128)}, u32[]{:S(2)}) copy-start(s32[40,8]{1,0:T(8,128)} %copy-done.15) | copy-start | bytes 3844
  75.2 6.1 %copy-start.12 = (s32[40,64]{0,1:T(8,128)S(1)}, s32[40,64]{0,1:T(8,128)}, u32[]{:S(2)}) copy-start(s32[40,64]{0,1:T(8,128)} %copy-done.11) | copy-start | bytes 30724
  77.1 4.4 %copy-start.24 = (f32[40,8]{0,1:T(8,128)S(1)}, f32[40,8]{0,1:T(8,128)}, u32[]{:S(2)}) copy-start(f32[40,8]{0,1:T(8,128)} %param.20) | copy-start | bytes 3844
  77.1 4.4 %copy-start.14 = (s32[40,8]{1,0:T(8,128)S(1)}, s32[40,8]{1,0:T(8,128)}, u32[]{:S(2)}) copy-start(s32[40,8]{1,0:T(8,128)} %copy-done.13) | copy-start | bytes 3844
  77.1 27.7 %all-to-all-start.3 = ((bf16[32,2,7,1024]{3,1,2,0:T(2,128)(2,1)}), bf16[32,2,7,1024]{3,1,2,0:T(2,128)(2,1)S(1)}, u32[]{:S(2)}, u32[]{:S(2)}) async-start(bf16[32,2,7,1024]{3,1,2,0:T(2,128)(2,1)} %copy.78), calls=%async_computation.3 | async-start | bytes 1835008 | tf_op jit(solution)/shard_map/all_to_all | solution.py:92
  81.8 29.2 %copy-start.10 = (s32[40,64]{0,1:T(8,128)S(1)}, s32[40,64]{0,1:T(8,128)}, u32[]{:S(2)}) copy-start(s32[40,64]{0,1:T(8,128)} %copy-done.9) | copy-start | bytes 30724
  81.8 30.0 %copy-start.20 = (s32[256]{0:T(256)S(1)}, s32[256]{0:T(256)}, u32[]{:S(2)}) copy-start(s32[256]{0:T(256)} %param.28) | copy-start | bytes 3076
  81.8 30.4 %copy-start.28 = (u32[256]{0:T(256)S(1)}, u32[256]{0:T(256)}, u32[]{:S(2)}) copy-start(u32[256]{0:T(256)} %constant.68) | copy-start | bytes 3076
  81.8 31.6 %copy-start.27 = (s32[40]{0:T(128)S(1)}, s32[40]{0:T(128)}, u32[]{:S(2)}) copy-start(s32[40]{0:T(128)} %param.27) | copy-start | bytes 484
  104.8 32.7 %all-to-all-start.2 = ((bf16[32,2,7,1024]{3,1,2,0:T(2,128)(2,1)}), bf16[32,2,7,1024]{3,1,2,0:T(2,128)(2,1)S(1)}, u32[]{:S(2)}, u32[]{:S(2)}) async-start(bf16[32,2,7,1024]{3,1,2,0:T(2,128)(2,1)} %copy.74), calls=%async_computation.2 | async-start | bytes 1835008 | tf_op jit(solution)/shard_map/all_to_all | solution.py:91
  137.5 1.2 copy-start.3
  137.5 1.2 copy-start.6
  137.8 1.6 copy-start.8
  138.7 2.4 copy-start.21
  195.3 13.5 %copy-start.17 = (s32[9728]{0:T(1024)S(1)}, s32[9728]{0:T(1024)}, u32[]{:S(2)}) copy-start(s32[9728]{0:T(1024)} %iota_add_fusion) | copy-start | bytes 116740
  208.8 66.7 %copy-start.26 = (s32[256]{0:T(256)S(1)}, s32[256]{0:T(256)}, u32[]{:S(2)}) copy-start(s32[256]{0:T(256)} %get-tuple-element.67) | copy-start | bytes 3076
  208.8 66.7 %copy-start.29 = (s32[40]{0:T(128)S(1)}, s32[40]{0:T(128)}, u32[]{:S(2)}) copy-start(s32[40]{0:T(128)} %iota_add_fusion.1) | copy-start | bytes 484
  208.8 173.4 %copy-start.25 = (s32[256]{0:T(256)S(1)}, s32[256]{0:T(256)}, u32[]{:S(2)}) copy-start(s32[256]{0:T(256)} %param.29) | copy-start | bytes 3076
  208.8 174.0 %copy-start.1 = (bf16[2,384,1024]{2,1,0:T(8,128)(2,1)S(1)}, bf16[2,384,1024]{2,1,0:T(8,128)(2,1)}, u32[]{:S(2)}) copy-start(bf16[2,384,1024]{2,1,0:T(8,128)(2,1)} %param.24) | copy-start | bytes 4718596
Sparse Core Ops, SparseCore 0:
  10.6 105.0 all-gather.3
where the time goes:
time: 391 us; the launch traced here: 390 us
  blocking collectives  222 us (57%)
  waiting for transfers between devices  49.2 us (13%)
  matrix products  38.7 us (10%)
  local copies, waits for them, and re-layouts  24.4 us (6%)
  starting transfers between devices  24.2 us (6%)
  other arithmetic  16.1 us (4%)
  between operations  15.3 us (4%)
    psum x1, blocking collectives, local(): sums = lax.psum(partial_value, ('grp', 'ep'))  107 us
    all_gather x3, blocking collectives, joined_2(): pieces = jax.tree.map(lambda part: lax.all_gather(part, axis), value)  54 us
    dot_general x2, matrix products, vocab_stats(): jnp.einsum('td,vd->tv', row_block, weights, preferred_element_type=jnp.fl...  26.9 us
    all_to_all x1, waiting for transfers between devices, local(): lax.all_to_all(outputs[:, :, slots:], 'ep', split_axis=0, concat_axis=0,...  21.1 us
    all_gather x1, blocking collectives, local(): lax.all_gather(ref_normed, 'grp', axis=0, tiled=True)  20.5 us
    unnamed x1, blocking collectives  20.4 us
    all_gather x1, blocking collectives, local(): lax.all_gather(pol_normed, 'grp', axis=0, tiled=True)  20.2 us
    all_to_all x1, waiting for transfers between devices, local(): lax.all_to_all(ref_send, 'ep', split_axis=0, concat_axis=0, tiled=True)  14.5 us
  transfers between devices with their start and end apart: 5, of which 3 were waited for; matrix products, arithmetic and copies ran while one was open for 9% of the time, Pallas kernels for 0%

commit v1 on v0

--- a/solution.py
+++ b/solution.py
@@ -133,7 +133,7 @@
     partial_value = jnp.dot(
         token_ratio, inside.astype(jnp.float32), precision=lax.Precision.HIGHEST
     ) / seq_lengths.astype(jnp.float32)
-    sums = lax.psum(partial_value, ("grp", "ep"))
+    sums = jnp.sum(lax.all_gather(partial_value, ("grp", "ep")), axis=0)
     owned = jnp.sum(jnp.where(owners == device_index, sums, 0.0)).reshape(1)
     return (token_ratio, owned)
 

time: 391 us -> 379 us (0.969)
  blocking collectives: 222 us -> 210 us
    psum x1 -> x0, blocking collectives: 107 us -> none  [local(): sums = lax.psum(partial_value, ('grp', 'ep'))]
    all_gather x0 -> x1, blocking collectives: none -> 94.4 us  [local(): sums = jnp.sum(lax.all_gather(partial_value, ('grp', 'ep')), axis=0)]
where the time goes in v1:
time: 379 us; the launch traced here: 378 us
  blocking collectives  210 us (55%)
  waiting for transfers between devices  49.2 us (13%)
  matrix products  38.7 us (10%)
  local copies, waits for them, and re-layouts  24.4 us (6%)
  starting transfers between devices  24.2 us (6%)
  other arithmetic  16.4 us (4%)
  between operations  15.3 us (4%)
    all_gather x1, blocking collectives, local(): sums = jnp.sum(lax.all_gather(partial_value, ('grp', 'ep')), axis=0)  94.4 us
    all_gather x3, blocking collectives, joined_2(): pieces = jax.tree.map(lambda part: lax.all_gather(part, axis), value)  54 us
    dot_general x2, matrix products, vocab_stats(): jnp.einsum('td,vd->tv', row_block, weights, preferred_element_type=jnp.fl...  26.9 us
    all_to_all x1, waiting for transfers between devices, local(): lax.all_to_all(outputs[:, :, slots:], 'ep', split_axis=0, concat_axis=0,...  21.1 us
    all_gather x1, blocking collectives, local(): lax.all_gather(ref_normed, 'grp', axis=0, tiled=True)  20.5 us
    unnamed x1, blocking collectives  20.4 us
    all_gather x1, blocking collectives, local(): lax.all_gather(pol_normed, 'grp', axis=0, tiled=True)  20.2 us
    all_to_all x1, waiting for transfers between devices, local(): lax.all_to_all(ref_send, 'ep', split_axis=0, concat_axis=0, tiled=True)  14.5 us
  transfers between devices with their start and end apart: 5, of which 3 were waited for; matrix products, arithmetic and copies ran while one was open for 9% of the time, Pallas kernels for 0%

profile of v1, /device:TPU:1, one launch (start us, length us, event | category | flops | bytes accessed | tf_op | source)
XLA Modules:
  0.0 377.9 jit_solution(11157705221089676749)
XLA Ops:
  7.2 0.7 all-gather.6.cloned.1.call-update
  7.9 0.8 copy.62
  8.9 0.4 copy-done.13
  9.4 0.6 copy-done.9
  10.4 0.6 copy-done.18
  11.0 0.4 convolution_convert_fusion.1
  11.8 2.0 copy.67
  13.7 8.7 %all-to-all-start = ((bf16[32,2,7,1024]{3,1,2,0:T(2,128)(2,1)}), bf16[32,2,7,1024]{3,1,2,0:T(2,128)(2,1)S(1)}, u32[]{:S(2)}, u32[]{:S(2)}) async-start(bf16[32,2,7,1024]{3,1,2,0:T(2,128)(2,1)} %copy.67), calls=%async_computation | async-start | bytes 1835008 | tf_op jit(solution)/shard_map/all_to_all | solution.py:81
  22.7 0.4 copy-done.15
  23.2 0.6 copy-done.11
  24.1 1.4 convolution_convert_fusion
  25.5 1.4 reshape.318
  27.0 2.0 copy.71
  28.9 12.9 %all-to-all-done = bf16[32,2,7,1024]{3,1,2,0:T(2,128)(2,1)S(1)} async-done(((bf16[32,2,7,1024]{3,1,2,0:T(2,128)(2,1)}), bf16[32,2,7,1024]{3,1,2,0:T(2,128)(2,1)S(1)}, u32[]{:S(2)}, u32[]{:S(2)}) %all-to-all-start) | async-done | bytes 917536 | tf_op jit(solution)/shard_map/all_to_all | solution.py:81
  41.8 0.9 copy-done.2
  42.7 5.4 %all-to-all-start.1 = ((bf16[32,2,7,1024]{3,1,2,0:T(2,128)(2,1)}), bf16[32,2,7,1024]{3,1,2,0:T(2,128)(2,1)}, u32[]{:S(2)}, u32[]{:S(2)}) async-start(bf16[32,2,7,1024]{3,1,2,0:T(2,128)(2,1)} %copy.71), calls=%async_computation.1 | async-start | bytes 1835008 | tf_op jit(solution)/shard_map/all_to_all | solution.py:82
  48.2 1.4 copy_dynamic-update-slice_fusion.1
  49.6 14.5 %all-to-all-done.1 = bf16[32,2,7,1024]{3,1,2,0:T(2,128)(2,1)} async-done(((bf16[32,2,7,1024]{3,1,2,0:T(2,128)(2,1)}), bf16[32,2,7,1024]{3,1,2,0:T(2,128)(2,1)}, u32[]{:S(2)}, u32[]{:S(2)}) %all-to-all-start.1) | async-done | bytes 917536 | tf_op jit(solution)/shard_map/all_to_all | solution.py:82
  64.1 1.5 copy_dynamic-update-slice_fusion
  65.8 2.2 fusion.9
  68.0 5.2 %convert_bitcast_fusion = bf16[32,2,14,1024]{3,0,2,1:T(8,128)(2,1)} fusion(bf16[2,384,1024]{2,1,0:T(8,128)(2,1)S(1)} %copy-done, bf16[32,2,14,1024]{3,0,2,1:T(8,128)(2,1)S(1)} %copy_dynamic-update-slice_fusion, bf16[2,1024,384]{2,1,0:T(8,128)(2,1)} %param.23, f32[32,2,14,384]{3,0,2,1:T(8,128)} %fusion.9), kind=kOutput, calls=%fused_computation.12 | convolution fusion | flops 1412268032 | bytes 8192000 | tf_op jit(solution)/shard_map/nesf,efd->nesd/dot_general | solution.py:88
  73.2 1.9 fusion.44
  75.2 1.9 copy.78
  77.1 3.9 %all-to-all-start.3 = ((bf16[32,2,7,1024]{3,1,2,0:T(2,128)(2,1)}), bf16[32,2,7,1024]{3,1,2,0:T(2,128)(2,1)S(1)}, u32[]{:S(2)}, u32[]{:S(2)}) async-start(bf16[32,2,7,1024]{3,1,2,0:T(2,128)(2,1)} %copy.78), calls=%async_computation.3 | async-start | bytes 1835008 | tf_op jit(solution)/shard_map/all_to_all | solution.py:92
  81.8 1.9 copy.74
  83.7 21.1 %all-to-all-done.3 = bf16[32,2,7,1024]{3,1,2,0:T(2,128)(2,1)S(1)} async-done(((bf16[32,2,7,1024]{3,1,2,0:T(2,128)(2,1)}), bf16[32,2,7,1024]{3,1,2,0:T(2,128)(2,1)S(1)}, u32[]{:S(2)}, u32[]{:S(2)}) %all-to-all-start.3) | async-done | bytes 917536 | tf_op jit(solution)/shard_map/all_to_all | solution.py:92
  104.8 6.1 %all-to-all-start.2 = ((bf16[32,2,7,1024]{3,1,2,0:T(2,128)(2,1)}), bf16[32,2,7,1024]{3,1,2,0:T(2,128)(2,1)S(1)}, u32[]{:S(2)}, u32[]{:S(2)}) async-start(bf16[32,2,7,1024]{3,1,2,0:T(2,128)(2,1)} %copy.74), calls=%async_computation.2 | async-start | bytes 1835008 | tf_op jit(solution)/shard_map/all_to_all | solution.py:91
  111.0 0.7 mul.94
  112.2 0.6 dynamic-slice
  113.7 20.4 %all-reduce = s32[320]{0:T(512)S(1)} all-reduce(s32[320]{0:T(512)S(1)} %dynamic-update-slice), channel_id=1, replica_groups=mesh['grp'=8,'ep'=32] {'grp'}, use_global_device_ids=true, to_apply=%add | all-reduce | flops 320 | bytes 2560
  134.0 0.6 iota_add_fusion.1
  134.7 0.6 fusion.43
  135.4 0.6 iota_add_fusion
  136.3 1.2 reshape.320
  138.1 0.6 copy-done.3
  138.7 0.7 multiply_reduce_fusion
  139.4 1.7 multiply_reduce_fusion.1
  141.2 20.2 %all_gather.32 = bf16[320,1024]{1,0:T(8,128)(2,1)S(1)} all-gather(bf16[40,1024]{1,0:T(8,128)(2,1)S(1)} %get-tuple-element.71), channel_id=1, replica_groups=mesh['grp'=8,'ep'=32] {'grp'}, dimensions={0}, use_global_device_ids=true | all-gather | bytes 737280 | tf_op jit(solution)/shard_map/all_gather | solution.py:107
  161.4 20.5 %all_gather.34 = bf16[320,1024]{1,0:T(8,128)(2,1)S(1)} all-gather(bf16[40,1024]{1,0:T(8,128)(2,1)S(1)} %get-tuple-element.72), channel_id=1, replica_groups=mesh['grp'=8,'ep'=32] {'grp'}, dimensions={0}, use_global_device_ids=true | all-gather | bytes 737280 | tf_op jit(solution)/shard_map/all_gather | solution.py:108
  181.9 13.4 %fusion.45 = (f32[320]{0:T(512)S(1)}, f32[320,9728]{1,0:T(8,128)}) fusion(bf16[320,1024]{1,0:T(8,128)(2,1)S(1)} %all_gather.32, bf16[9728,1024]{1,0:T(8,128)(2,1)} %all-gather.6.cloned.1.call-done), kind=kOutput, calls=%fused_computation.84 | convolution fusion | flops 6378454528 | bytes 33031424 | tf_op jit(solution)/shard_map/td,vd->tv/dot_general | solution.py:24
  195.3 13.5 %fusion.46 = (f32[320]{0:T(512)S(1)}, f32[320,9728]{1,0:T(8,128)}) fusion(bf16[320,1024]{1,0:T(8,128)(2,1)S(1)} %all_gather.34, bf16[9728,1024]{1,0:T(8,128)(2,1)} %all-gather.6.cloned.1.call-done), kind=kOutput, calls=%fused_computation.85 | convolution fusion | flops 6378454528 | bytes 33031424 | tf_op jit(solution)/shard_map/td,vd->tv/dot_general | solution.py:24
  208.8 11.5 %fusion.2 = (f32[320]{0:T(512)S(1)}, f32[320]{0:T(512)S(1)}, f32[320]{0:T(512)S(1)}, f32[320]{0:T(512)S(1)}) fusion(f32[320,9728]{1,0:T(8,128)} %get-tuple-element.80, s32[9728]{0:T(1024)S(1)} %copy-done.17, s32[320]{0:T(512)S(1)} %all-reduce, f32[320]{0:T(512)S(1)} %get-tuple-element.79, f32[320,9728]{1,0:T(8,128)} %get-tuple-element.82, ...), kind=kLoop, calls=%fused_computation.8 | loop fusion | flops 28015360 | bytes 24951552 | tf_op jit(solution)/shard_map/reduce_sum | solution.py:27
  220.3 18.0 %all-gather.2 = f32[8,2,320]{2,1,0:T(2,128)S(1)} all-gather(f32[1,2,320]{2,1,0:T(2,128)S(1)} %maximum_bitcast_fusion), channel_id=2, replica_groups=mesh['grp'=8,'ep'=32] {'grp'}, dimensions={0}, use_global_device_ids=true | all-gather | bytes 23040 | tf_op jit(solution)/shard_map/all_gather | solution.py:8
  238.4 18.0 %all_gather.36 = f32[8,2,320]{2,1,0:T(2,128)S(1)} all-gather(f32[1,2,320]{2,1,0:T(2,128)S(1)} %get-tuple-element.73), channel_id=1, replica_groups=mesh['grp'=8,'ep'=32] {'grp'}, dimensions={0}, use_global_device_ids=true | all-gather | bytes 23040 | tf_op jit(solution)/shard_map/all_gather | solution.py:8
  256.5 18.0 %all_gather.35 = f32[8,2,320]{2,1,0:T(2,128)S(1)} all-gather(f32[1,2,320]{2,1,0:T(2,128)S(1)} %get-tuple-element.74), channel_id=1, replica_groups=mesh['grp'=8,'ep'=32] {'grp'}, dimensions={0}, use_global_device_ids=true | all-gather | bytes 23040 | tf_op jit(solution)/shard_map/all_gather | solution.py:8
  274.9 0.5 fusion.42
  275.7 94.4 %all-gather.3 = f32[256,1,256]{2,1,0:T(1,128)S(1)} all-gather(f32[1,1,256]{2,1,0:T(1,128)S(1)} %bitcast.99), channel_id=3, replica_groups=mesh['grp'=8,'ep'=32] {'grp','ep'}, dimensions={0}, use_global_device_ids=true | all-gather | bytes 263168 | tf_op jit(solution)/shard_map/all_gather | solution.py:136
  370.4 0.6 fusion.39
  (126 shorter events, 5.6 us)
Async XLA Ops:
  7.2 60.8 %copy-start = (bf16[2,384,1024]{2,1,0:T(8,128)(2,1)S(1)}, bf16[2,384,1024]{2,1,0:T(8,128)(2,1)}, u32[]{:S(2)}) copy-start(bf16[2,384,1024]{2,1,0:T(8,128)(2,1)} %param.24) | copy-start | bytes 4718596
  7.2 3.8 %copy-start.7 = (bf16[40,1024]{1,0:T(8,128)(2,1)S(1)}, bf16[40,1024]{1,0:T(8,128)(2,1)}, u32[]{:S(2)}) copy-start(bf16[40,1024]{1,0:T(8,128)(2,1)} %param.16) | copy-start | bytes 245764
  7.2 174.7 %all-gather.6.cloned.1.call-start = ((), (), s32[]{:S(2)}) async-start(), calls=%async_computation.4 | async-start | bytes 20545536 | tf_op jit(solution)/shard_map/all_gather | solution.py:114
  8.7 0.6 copy-start.13
  9.4 0.6 copy-start.9
  10.4 0.6 copy-start.18
  11.7 10.7 %copy-start.22 = (s32[40,8]{0,1:T(8,128)S(1)}, s32[40,8]{0,1:T(8,128)}, u32[]{:S(2)}) copy-start(s32[40,8]{0,1:T(8,128)} %param.19) | copy-start | bytes 3844
  13.7 10.4 %copy-start.5 = (bf16[40,1024]{1,0:T(8,128)(2,1)S(1)}, bf16[40,1024]{1,0:T(8,128)(2,1)}, u32[]{:S(2)}) copy-start(bf16[40,1024]{1,0:T(8,128)(2,1)} %param.17) | copy-start | bytes 245764
  13.7 10.4 %copy-start.19 = (s32[448]{0:T(512)S(1)}, s32[448]{0:T(512)}, u32[]{:S(2)}) copy-start(s32[448]{0:T(512)} %copy-done.18) | copy-start | bytes 5380
  13.7 28.1 %all-to-all-start = ((bf16[32,2,7,1024]{3,1,2,0:T(2,128)(2,1)}), bf16[32,2,7,1024]{3,1,2,0:T(2,128)(2,1)S(1)}, u32[]{:S(2)}, u32[]{:S(2)}) async-start(bf16[32,2,7,1024]{3,1,2,0:T(2,128)(2,1)} %copy.67), calls=%async_computation | async-start | bytes 1835008 | tf_op jit(solution)/shard_map/all_to_all | solution.py:81
  22.5 0.6 copy-start.15
  23.2 0.6 copy-start.11
  41.8 0.9 copy-start.2
  42.7 21.4 %all-to-all-start.1 = ((bf16[32,2,7,1024]{3,1,2,0:T(2,128)(2,1)}), bf16[32,2,7,1024]{3,1,2,0:T(2,128)(2,1)}, u32[]{:S(2)}, u32[]{:S(2)}) async-start(bf16[32,2,7,1024]{3,1,2,0:T(2,128)(2,1)} %copy.71), calls=%async_computation.1 | async-start | bytes 1835008 | tf_op jit(solution)/shard_map/all_to_all | solution.py:82
  64.1 1.7 copy-start.4
  75.2 5.8 %copy-start.23 = (f32[40,8]{0,1:T(8,128)S(1)}, f32[40,8]{0,1:T(8,128)}, u32[]{:S(2)}) copy-start(f32[40,8]{0,1:T(8,128)} %param.21) | copy-start | bytes 3844
  75.2 5.9 %copy-start.16 = (s32[40,8]{1,0:T(8,128)S(1)}, s32[40,8]{1,0:T(8,128)}, u32[]{:S(2)}) copy-start(s32[40,8]{1,0:T(8,128)} %copy-done.15) | copy-start | bytes 3844
  75.2 6.1 %copy-start.12 = (s32[40,64]{0,1:T(8,128)S(1)}, s32[40,64]{0,1:T(8,128)}, u32[]{:S(2)}) copy-start(s32[40,64]{0,1:T(8,128)} %copy-done.11) | copy-start | bytes 30724
  77.1 4.4 %copy-start.24 = (f32[40,8]{0,1:T(8,128)S(1)}, f32[40,8]{0,1:T(8,128)}, u32[]{:S(2)}) copy-start(f32[40,8]{0,1:T(8,128)} %param.20) | copy-start | bytes 3844
  77.1 4.4 %copy-start.14 = (s32[40,8]{1,0:T(8,128)S(1)}, s32[40,8]{1,0:T(8,128)}, u32[]{:S(2)}) copy-start(s32[40,8]{1,0:T(8,128)} %copy-done.13) | copy-start | bytes 3844
  77.1 27.7 %all-to-all-start.3 = ((bf16[32,2,7,1024]{3,1,2,0:T(2,128)(2,1)}), bf16[32,2,7,1024]{3,1,2,0:T(2,128)(2,1)S(1)}, u32[]{:S(2)}, u32[]{:S(2)}) async-start(bf16[32,2,7,1024]{3,1,2,0:T(2,128)(2,1)} %copy.78), calls=%async_computation.3 | async-start | bytes 1835008 | tf_op jit(solution)/shard_map/all_to_all | solution.py:92
  81.8 29.2 %copy-start.10 = (s32[40,64]{0,1:T(8,128)S(1)}, s32[40,64]{0,1:T(8,128)}, u32[]{:S(2)}) copy-start(s32[40,64]{0,1:T(8,128)} %copy-done.9) | copy-start | bytes 30724
  81.8 30.0 %copy-start.20 = (s32[256]{0:T(256)S(1)}, s32[256]{0:T(256)}, u32[]{:S(2)}) copy-start(s32[256]{0:T(256)} %param.28) | copy-start | bytes 3076
  81.8 30.4 %copy-start.28 = (u32[256]{0:T(256)S(1)}, u32[256]{0:T(256)}, u32[]{:S(2)}) copy-start(u32[256]{0:T(256)} %constant.68) | copy-start | bytes 3076
  81.8 31.6 %copy-start.27 = (s32[40]{0:T(128)S(1)}, s32[40]{0:T(128)}, u32[]{:S(2)}) copy-start(s32[40]{0:T(128)} %param.27) | copy-start | bytes 484
  104.8 32.7 %all-to-all-start.2 = ((bf16[32,2,7,1024]{3,1,2,0:T(2,128)(2,1)}), bf16[32,2,7,1024]{3,1,2,0:T(2,128)(2,1)S(1)}, u32[]{:S(2)}, u32[]{:S(2)}) async-start(bf16[32,2,7,1024]{3,1,2,0:T(2,128)(2,1)} %copy.74), calls=%async_computation.2 | async-start | bytes 1835008 | tf_op jit(solution)/shard_map/all_to_all | solution.py:91
  137.5 1.2 copy-start.3
  137.5 1.2 copy-start.6
  137.8 1.6 copy-start.8
  138.7 2.4 copy-start.21
  195.3 13.5 %copy-start.17 = (s32[9728]{0:T(1024)S(1)}, s32[9728]{0:T(1024)}, u32[]{:S(2)}) copy-start(s32[9728]{0:T(1024)} %iota_add_fusion) | copy-start | bytes 116740
  208.8 66.7 %copy-start.26 = (s32[256]{0:T(256)S(1)}, s32[256]{0:T(256)}, u32[]{:S(2)}) copy-start(s32[256]{0:T(256)} %get-tuple-element.67) | copy-start | bytes 3076
  208.8 66.7 %copy-start.29 = (s32[40]{0:T(128)S(1)}, s32[40]{0:T(128)}, u32[]{:S(2)}) copy-start(s32[40]{0:T(128)} %iota_add_fusion.1) | copy-start | bytes 484
  208.8 161.6 %copy-start.25 = (s32[256]{0:T(256)S(1)}, s32[256]{0:T(256)}, u32[]{:S(2)}) copy-start(s32[256]{0:T(256)} %param.29) | copy-start | bytes 3076
  208.8 162.2 %copy-start.1 = (bf16[2,384,1024]{2,1,0:T(8,128)(2,1)S(1)}, bf16[2,384,1024]{2,1,0:T(8,128)(2,1)}, u32[]{:S(2)}) copy-start(bf16[2,384,1024]{2,1,0:T(8,128)(2,1)} %param.24) | copy-start | bytes 4718596
Sparse Core Ops, SparseCore 0:
  10.6 105.0 all-gather.5
